TPU v7x, 32 devices: a whole 2x2x4 slice. The times are simulated.
32 devices in a mesh: section: 2 (over core), req: 4 (over z), head: 4 (over y, x).
Axes of the slice: x: 2, y: 2, z: 4, core: 2. Of those that a mesh axis runs over, the one named last changes fastest.
Arguments:
- tokens: bfloat16 [128, 1024], P('req'), may hold values from -60 to 60, as said below
- deal: int32 [128], P('req'), may hold values from 0 to 127, each once
- lengths: int32 [2, 128], P('section', 'req'), may hold values from 2 to 256, as said below
- cache_keys: bfloat16 [2, 128, 256, 1024], P('section', 'req', None, 'head'), may hold values from -1024 to 1024
- cache_values: bfloat16 [2, 128, 256, 1024], P('section', 'req', None, 'head'), may hold values from -6 to 6
- w_qkv: bfloat16 [2, 1024, 3, 1024], P('section', None, None, 'head'), may hold values from -0.1875 to 0.1875
- w_out: bfloat16 [2, 1024, 1024], P('section', 'head'), may hold values from -0.1875 to 0.1875
- attn_gain: float32 [2, 1024], P('section'), may hold values from 0.5 to 1.5
- ffn_gain: float32 [2, 1024], P('section'), may hold values from 0.5 to 1.5
- w_gate: bfloat16 [2, 1024, 45056], P('section', None, ('req', 'head')), may hold values from -0.1875 to 0.1875
- w_up: bfloat16 [2, 1024, 45056], P('section', None, ('req', 'head')), may hold values from -0.1875 to 0.1875
- w_down: bfloat16 [2, 45056, 1024], P('section', ('req', 'head')), may hold values from -0.109375 to 0.109375
- routes: int32 [2, 128, 2], P('section', 'req'), may hold values from 0 to 15, all different within a row; in each aligned block of 16 rows (0 to 15, 16 to 31, ..., all dimensions but the last counted through in order) at most 4 rows name the same one
- gates: bfloat16 [2, 128, 2], P('section', 'req'), may hold values from 0.25 to 1
Outputs:
- layer_out: bfloat16 [2, 128, 1024], P('section', 'req')
Inputs may be any that keep to these rules, and one draw needn't show every extreme that they name: `tokens`: hidden states with row and feature scales that differ. `deal`: each of 0 to 127 appears once. `lengths`: in each layer, one of the 32 slots of each index of req holds a length of exactly 256; the others are anywhere from 2 to 256. `routes`: the two experts of a slot differ; in each aligned block of 16 slots of one layer no expert is named more than 4 times.
All inputs are finite; a program needn't handle non-finite values.
Results may differ from a plain program's by a relative error of at most 0.0053.
Values may be sent and summed in bfloat16 or wider, within the bound.
A program may use at most 128 MiB of HBM per device.

v0:
```python
import math

import jax
import jax.numpy as jnp
from jax import lax
from jax.sharding import PartitionSpec as P

HEAD_DIM = 64
EXPERTS = 16
FF = 2816
MICRO = 2


epsilon = 1e-06


def shifted(x, axis, by):
    size = lax.axis_size(axis)
    pairs = [(i, i + by) for i in range(size) if 0 <= i + by < size]
    return lax.ppermute(x, axis, pairs)


def rms_scale(values, gain_row):
    mean_square = jnp.mean(values * values, axis=-1, keepdims=True)
    return values * lax.rsqrt(mean_square + epsilon) * gain_row


def attend_block(queries, new_keys, new_values, key_cache, value_cache, lengths):
    score_scale = 1.0 / math.sqrt(queries.shape[-1])
    scores = (
        jnp.einsum("bhd,bjhd->bhj", queries, key_cache, preferred_element_type=jnp.float32)
        * score_scale
    )
    own_score = (
        jnp.sum(queries.astype(jnp.float32) * new_keys.astype(jnp.float32), axis=-1) * score_scale
    )
    positions = jnp.arange(key_cache.shape[1], dtype=jnp.int32)
    in_range = positions[None, None, :] < lengths[:, None, None]
    scores = jnp.where(in_range, scores, -jnp.inf)
    peak_score = jnp.maximum(jnp.max(scores, axis=-1), own_score)
    cache_weight = jnp.exp(scores - peak_score[..., None])
    own_weight = jnp.exp(own_score - peak_score)
    denominator = jnp.sum(cache_weight, axis=-1) + own_weight
    cache_prob = (cache_weight / denominator[..., None]).astype(jnp.bfloat16)
    own_prob = (own_weight / denominator).astype(jnp.bfloat16)
    attended = jnp.einsum(
        "bhj,bjhd->bhd", cache_prob, value_cache, preferred_element_type=jnp.float32
    )
    attended = attended + own_prob.astype(jnp.float32)[..., None] * new_values.astype(jnp.float32)
    return attended.astype(jnp.bfloat16)


def on_device(
    tokens,
    deal,
    lengths,
    cache_keys,
    cache_values,
    w_qkv,
    w_out,
    attn_gain,
    ffn_gain,
    w_gate,
    w_up,
    w_down,
    routes,
    gates,
):
    req_count = lax.axis_size("req")
    head_count = lax.axis_size("head")
    section_index = lax.axis_index("section")
    request_slots = tokens.shape[0]
    model_width = tokens.shape[1]
    block_rows = request_slots // MICRO
    unit_count = w_gate.shape[2]
    head_cols = w_out.shape[1]
    heads_here = head_cols // HEAD_DIM
    context = cache_keys.shape[2]
    expert_ids = jnp.arange(EXPERTS, dtype=jnp.int32)
    own_expert = (lax.axis_index("req") * head_count + lax.axis_index("head")) * unit_count // FF
    qkv_weight = w_qkv[0].reshape(model_width, 3 * head_cols)
    everything = lax.all_gather(tokens, "req", axis=0, tiled=True)
    dealt_rows = jnp.take(everything, deal, axis=0)
    results = jnp.zeros((request_slots, model_width), jnp.bfloat16)
    incoming = jnp.zeros((block_rows, model_width), jnp.bfloat16)
    for tick_index in range(MICRO + 1):
        micro_index = tick_index - section_index
        in_window = (micro_index >= 0) & (micro_index < MICRO)
        clamped = jnp.clip(micro_index, 0, MICRO - 1)
        fresh_rows = lax.dynamic_slice_in_dim(dealt_rows, clamped * block_rows, block_rows, 0)
        hidden_in = jnp.where(section_index == 0, fresh_rows, incoming)
        row_start = clamped * block_rows
        lengths_here = lax.dynamic_slice_in_dim(lengths[0], row_start, block_rows, 0)
        key_cache = lax.dynamic_slice_in_dim(cache_keys[0], row_start, block_rows, 0).reshape(
            block_rows, context, heads_here, HEAD_DIM
        )
        value_cache = lax.dynamic_slice_in_dim(cache_values[0], row_start, block_rows, 0).reshape(
            block_rows, context, heads_here, HEAD_DIM
        )
        route_ids = lax.dynamic_slice_in_dim(routes[0], row_start, block_rows, 0)
        gate_vals = lax.dynamic_slice_in_dim(gates[0], row_start, block_rows, 0)
        normed = rms_scale(hidden_in.astype(jnp.float32), attn_gain[0]).astype(jnp.bfloat16)
        projected = jnp.dot(normed, qkv_weight, preferred_element_type=jnp.float32).astype(
            jnp.bfloat16
        )
        queries = projected[:, :head_cols].reshape(block_rows, heads_here, HEAD_DIM)
        new_keys = projected[:, head_cols : 2 * head_cols].reshape(block_rows, heads_here, HEAD_DIM)
        new_values = projected[:, 2 * head_cols :].reshape(block_rows, heads_here, HEAD_DIM)
        attended = attend_block(
            queries, new_keys, new_values, key_cache, value_cache, lengths_here
        ).reshape(block_rows, head_cols)
        partial_value = jnp.dot(attended, w_out[0], preferred_element_type=jnp.float32)
        attention = lax.psum(partial_value, "head")
        residual = hidden_in.astype(jnp.float32) + attention
        normed_ffn = rms_scale(residual, ffn_gain[0]).astype(jnp.bfloat16)
        bf_zero = jnp.zeros((), jnp.bfloat16)
        combine = jnp.sum(
            jnp.where(
                route_ids[:, :, None] == expert_ids[None, None, :], gate_vals[:, :, None], bf_zero
            ),
            axis=1,
        )
        piece_tokens, piece_combine = lax.all_gather(
            (normed_ffn, combine), "req", axis=0, tiled=True
        )
        expert_row_weight = jnp.sum(
            jnp.where(expert_ids[None, :] == own_expert, piece_combine.astype(jnp.float32), 0.0),
            axis=1,
        )
        gate_part = jnp.dot(piece_tokens, w_gate[0], preferred_element_type=jnp.float32)
        up_part = jnp.dot(piece_tokens, w_up[0], preferred_element_type=jnp.float32)
        hidden = (
            expert_row_weight[:, None] * jax.nn.gelu(gate_part, approximate=True) * up_part
        ).astype(jnp.bfloat16)
        partial_terms = jnp.dot(hidden, w_down[0], preferred_element_type=jnp.float32)
        mixture = lax.psum_scatter(partial_terms, "req", scatter_dimension=0, tiled=True)
        mixture = lax.psum(mixture, "head")
        produced = (residual + mixture).astype(jnp.bfloat16)
        updated = lax.dynamic_update_slice_in_dim(results, produced, clamped * block_rows, 0)
        results = jnp.where(in_window, updated, results)
        if tick_index < MICRO:
            incoming = shifted(produced, "section", 1)
    placed = (
        jnp.zeros((request_slots * req_count, model_width), jnp.float32)
        .at[deal]
        .set(results.astype(jnp.float32))
    )
    initial_rows = lax.psum_scatter(
        placed.astype(jnp.bfloat16), "req", scatter_dimension=0, tiled=True
    )
    return initial_rows[None]


def solution(mesh):
    return jax.shard_map(
        on_device,
        mesh=mesh,
        in_specs=(
            P("req", None),
            P("req"),
            P("section", "req"),
            P("section", "req", None, "head"),
            P("section", "req", None, "head"),
            P("section", None, None, "head"),
            P("section", "head", None),
            P("section", None),
            P("section", None),
            P("section", None, ("req", "head")),
            P("section", None, ("req", "head")),
            P("section", ("req", "head"), None),
            P("section", "req", None),
            P("section", "req", None),
        ),
        out_specs=P("section", "req", None),
        check_vma=False,
    )
```

profile of v0, /device:TPU:1, one launch (start us, length us, event | category | flops | bytes accessed | tf_op | source)
XLA Modules:
  0.0 503.4 jit_solution(13057923560571487558)
XLA Ops:
  6.5 0.7 compare_select_fusion
  7.3 0.7 compare_and_fusion
  7.9 13.5 %all_gather.21 = bf16[128,1024]{1,0:T(8,128)(2,1)S(1)} all-gather(bf16[32,1024]{1,0:T(8,128)(2,1)} %param.14), channel_id=1, replica_groups=mesh['section'=2,'req'=4,'head'=4] {'req'}, dimensions={0}, use_global_device_ids=true | all-gather | bytes 327680 | tf_op jit(solution)/shard_map/all_gather | solution.py:82
  21.5 0.6 gather_fusion
  22.3 1.7 copy.47
  24.0 0.5 convolution_convert_fusion.2
  24.8 8.9 %constant_dynamic-slice_fusion.2 = (bf16[1,16,256,256]{3,2,1,0:T(8,128)(2,1)}, bf16[1,16,256,256]{3,2,1,0:T(8,128)(2,1)}, bf16[1,16,256,256]{3,2,1,0:T(8,128)(2,...) fusion(bf16[1,32,256,256]{3,2,1,0:T(8,128)(2,1)} %param.18, ...), kind=kLoop, calls=%fused_computation.162 | loop fusion | bytes 25165836 | tf_op jit(solution)/shard_map/dynamic_slice | solution.py:97
  33.7 3.9 copy.78
  38.0 2.0 fusion.146
  40.1 0.2 fusion.105
  40.4 3.9 copy.79
  44.5 2.2 fusion.103
  46.9 0.8 fusion.82
  48.1 10.2 %all_gather.22 = bf16[64,16]{1,0:T(8,128)(2,1)S(1)} all-gather(bf16[16,16]{1,0:T(8,128)(2,1)S(1)} %fusion.130), channel_id=1, replica_groups=mesh['section'=2,'req'=4,'head'=4] {'req'}, dimensions={0}, use_global_device_ids=true | all-gather | bytes 2560 | tf_op jit(solution)/shard_map/all_gather | solution.py:123
  58.4 10.2 %all_gather.24 = bf16[64,16]{1,0:T(8,128)(2,1)S(1)} all-gather(bf16[16,16]{1,0:T(8,128)(2,1)S(1)} %fusion.129), channel_id=1, replica_groups=mesh['section'=2,'req'=4,'head'=4] {'req'}, dimensions={0}, use_global_device_ids=true | all-gather | bytes 2560 | tf_op jit(solution)/shard_map/all_gather | solution.py:123
  68.7 10.2 %all_gather.26 = bf16[64,16]{1,0:T(8,128)(2,1)S(1)} all-gather(bf16[16,16]{1,0:T(8,128)(2,1)S(1)} %fusion.128), channel_id=1, replica_groups=mesh['section'=2,'req'=4,'head'=4] {'req'}, dimensions={0}, use_global_device_ids=true | all-gather | bytes 2560 | tf_op jit(solution)/shard_map/all_gather | solution.py:123
  79.0 13.6 %all-reduce.7.cloned.1.call-done = f32[16,1024]{1,0:T(8,128)} async-done(((f32[16,1024]{1,0:T(8,128)}), f32[16,1024]{1,0:T(8,128)}) %all-reduce.7.cloned.1.call-update) | async-done | bytes 65552 | tf_op jit(solution)/shard_map/psum | solution.py:113
  92.6 1.0 multiply_reduce_fusion.2
  93.6 0.9 multiply_convert_fusion.2
  94.5 10.9 %all_gather.23 = bf16[64,1024]{1,0:T(8,128)(2,1)S(1)} all-gather(bf16[16,1024]{1,0:T(8,128)(2,1)S(1)} %multiply_convert_fusion.2), channel_id=1, replica_groups=mesh['section'=2,'req'=4,'head'=4] {'req'}, dimensions={0}, use_global_device_ids=true | all-gather | bytes 163840 | tf_op jit(solution)/shard_map/all_gather | solution.py:123
  105.4 3.9 fusion.45
  109.2 7.2 %fusion.4 = f32[64,1024]{1,0:T(8,128)} fusion(bf16[1,2816,1024]{2,1,0:T(8,128)(2,1)} %param.25, f32[64,2816]{1,0:T(8,128)S(1)} %fusion.45, bf16[64,1024]{1,0:T(8,128)(2,1)S(1)} %all_gather.23, bf16[1,1024,2816]{2,1,0:T(8,128)(2,1)} %param.24), kind=kOutput, calls=%fused_computation.6 | convolution fusion | flops 738557952 | bytes 12648448 | tf_op jit(solution)/shard_map/dot_general | solution.py:135
  116.5 21.1 %reduce-scatter.5.cloned.1.call-done = f32[16,1024]{1,0:T(8,128)} async-done(((f32[64,1024]{1,0:T(8,128)}), f32[16,1024]{1,0:T(8,128)}) %reduce-scatter.5.cloned.1.call-update) | async-done | bytes 65552 | tf_op jit(solution)/shard_map/reduce_scatter | solution.py:136
  137.7 43.8 %all-reduce.9.cloned.1.call-done = f32[16,1024]{1,0:T(8,128)} async-done(((f32[16,1024]{1,0:T(8,128)}), f32[16,1024]{1,0:T(8,128)}) %all-reduce.9.cloned.1.call-update) | async-done | bytes 65552 | tf_op jit(solution)/shard_map/psum | solution.py:137
  181.5 0.9 select_dynamic-update-slice_fusion.1
  182.4 1.3 collective-permute-start
  183.8 3.9 copy.80
  187.7 3.9 copy.81
  191.6 0.1 fusion.90
  191.7 0.5 convolution_convert_fusion.1
  192.7 2.0 fusion.147
  194.8 0.2 fusion.106
  195.3 2.2 fusion.101
  197.7 0.8 fusion.80
  198.6 41.7 %all-reduce.11.cloned.1.call-done = f32[16,1024]{1,0:T(8,128)} async-done(((f32[16,1024]{1,0:T(8,128)}), f32[16,1024]{1,0:T(8,128)}) %all-reduce.11.cloned.1.call-update) | async-done | bytes 65552 | tf_op jit(solution)/shard_map/psum | solution.py:113
  240.2 1.0 multiply_reduce_fusion.1
  241.2 0.9 multiply_convert_fusion.1
  242.1 10.9 %all_gather.25 = bf16[64,1024]{1,0:T(8,128)(2,1)S(1)} all-gather(bf16[16,1024]{1,0:T(8,128)(2,1)S(1)} %multiply_convert_fusion.1), channel_id=1, replica_groups=mesh['section'=2,'req'=4,'head'=4] {'req'}, dimensions={0}, use_global_device_ids=true | all-gather | bytes 163840 | tf_op jit(solution)/shard_map/all_gather | solution.py:123
  253.0 3.9 fusion.57
  256.9 7.2 %fusion.2 = f32[64,1024]{1,0:T(8,128)} fusion(bf16[1,2816,1024]{2,1,0:T(8,128)(2,1)} %param.25, f32[64,2816]{1,0:T(8,128)S(1)} %fusion.57, bf16[64,1024]{1,0:T(8,128)(2,1)S(1)} %all_gather.25, bf16[1,1024,2816]{2,1,0:T(8,128)(2,1)} %param.24), kind=kOutput, calls=%fused_computation.4 | convolution fusion | flops 738557952 | bytes 12648448 | tf_op jit(solution)/shard_map/dot_general | solution.py:135
  264.1 21.1 %reduce-scatter.7.cloned.1.call-done = f32[16,1024]{1,0:T(8,128)} async-done(((f32[64,1024]{1,0:T(8,128)}), f32[16,1024]{1,0:T(8,128)}) %reduce-scatter.7.cloned.1.call-update) | async-done | bytes 65552 | tf_op jit(solution)/shard_map/reduce_scatter | solution.py:136
  285.3 43.9 %all-reduce.13.cloned.1.call-done = f32[16,1024]{1,0:T(8,128)} async-done(((f32[16,1024]{1,0:T(8,128)}), f32[16,1024]{1,0:T(8,128)}) %all-reduce.13.cloned.1.call-update) | async-done | bytes 65552 | tf_op jit(solution)/shard_map/psum | solution.py:137
  329.2 0.9 select_dynamic-update-slice_fusion
  330.1 1.5 collective-permute-start.1
  331.5 3.9 copy.82
  335.5 3.9 copy.83
  339.4 0.1 fusion.93
  339.5 0.5 convolution_convert_fusion
  340.5 2.1 fusion.148
  342.8 0.2 fusion.107
  343.3 0.6 fusion.99
  344.1 0.8 fusion.78
  345.0 41.6 %all-reduce.15.cloned.1.call-done = f32[16,1024]{1,0:T(8,128)} async-done(((f32[16,1024]{1,0:T(8,128)}), f32[16,1024]{1,0:T(8,128)}) %all-reduce.15.cloned.1.call-update) | async-done | bytes 65552 | tf_op jit(solution)/shard_map/psum | solution.py:113
  386.6 1.0 multiply_reduce_fusion
  387.6 0.9 multiply_convert_fusion
  388.5 10.9 %all_gather.27 = bf16[64,1024]{1,0:T(8,128)(2,1)S(1)} all-gather(bf16[16,1024]{1,0:T(8,128)(2,1)S(1)} %multiply_convert_fusion), channel_id=1, replica_groups=mesh['section'=2,'req'=4,'head'=4] {'req'}, dimensions={0}, use_global_device_ids=true | all-gather | bytes 163840 | tf_op jit(solution)/shard_map/all_gather | solution.py:123
  399.4 3.9 fusion.69
  403.2 7.2 %fusion = f32[64,1024]{1,0:T(8,128)} fusion(bf16[1,2816,1024]{2,1,0:T(8,128)(2,1)} %param.25, f32[64,2816]{1,0:T(8,128)S(1)} %fusion.69, bf16[64,1024]{1,0:T(8,128)(2,1)S(1)} %all_gather.27, bf16[1,1024,2816]{2,1,0:T(8,128)(2,1)} %param.24), kind=kOutput, calls=%fused_computation.2 | convolution fusion | flops 738557952 | bytes 12648448 | tf_op jit(solution)/shard_map/dot_general | solution.py:135
  410.5 21.1 %reduce-scatter.9.cloned.1.call-done = f32[16,1024]{1,0:T(8,128)} async-done(((f32[64,1024]{1,0:T(8,128)}), f32[16,1024]{1,0:T(8,128)}) %reduce-scatter.9.cloned.1.call-update) | async-done | bytes 65552 | tf_op jit(solution)/shard_map/reduce_scatter | solution.py:136
  431.7 43.8 %all-reduce.17.cloned.1.call-done = f32[16,1024]{1,0:T(8,128)} async-done(((f32[16,1024]{1,0:T(8,128)}), f32[16,1024]{1,0:T(8,128)}) %all-reduce.17.cloned.1.call-update) | async-done | bytes 65552 | tf_op jit(solution)/shard_map/psum | solution.py:137
  475.5 0.9 fusion.112
  476.4 0.8 scatter_custom_fusion
  477.2 0.7 convert_element_type.232
  478.0 18.6 %reduce-scatter.11.cloned.1.call-done = bf16[32,1024]{1,0:T(8,128)(2,1)} async-done(((bf16[128,1024]{1,0:T(8,128)(2,1)}), bf16[32,1024]{1,0:T(8,128)(2,1)}) %reduce-scatter.11.cloned.1.call-update) | async-done | bytes 65552 | tf_op jit(solution)/shard_map/reduce_scatter | solution.py:148
  (104 shorter events, 4.6 us)
Async XLA Ops:
  6.5 40.4 %copy-start = (bf16[1,256,1024]{2,1,0:T(8,128)(2,1)S(1)}, bf16[1,256,1024]{2,1,0:T(8,128)(2,1)}, u32[]{:S(2)}) copy-start(bf16[1,256,1024]{2,1,0:T(8,128)(2,1)} %param.20) | copy-start | bytes 1572868
  6.5 86.1 %all-reduce.7.cloned.1.call-start = ((), (), s32[]{:S(2)}) async-start(), calls=%async_computation.4 | async-start | bytes 131072 | tf_op jit(solution)/shard_map/psum | solution.py:113
  7.9 16.1 %copy-start.5 = (f32[1,1024]{1,0:T(1,128)S(1)}, f32[1,1024]{1,0:T(1,128)}, u32[]{:S(2)}) copy-start(f32[1,1024]{1,0:T(1,128)} %param.21) | copy-start | bytes 12292
  33.6 3.9 copy-start.8
  44.3 3.5 copy-start.7
  44.3 3.6 copy-start.9
  44.3 49.3 %copy-start.6 = (f32[1,1024]{1,0:T(1,128)S(1)}, f32[1,1024]{1,0:T(1,128)}, u32[]{:S(2)}) copy-start(f32[1,1024]{1,0:T(1,128)} %param.22) | copy-start | bytes 12292
  47.7 89.9 %reduce-scatter.5.cloned.1.call-start = ((), (), s32[]{:S(2)}) async-start(), calls=%async_computation.5 | async-start | bytes 327680 | tf_op jit(solution)/shard_map/reduce_scatter | solution.py:136
  109.2 72.3 %copy-start.2 = (f32[16,1024]{1,0:T(8,128)S(1)}, f32[16,1024]{1,0:T(8,128)}, u32[]{:S(2)}) copy-start(f32[16,1024]{1,0:T(8,128)} %all-reduce.7.cloned.1.call-done) | copy-start | bytes 196612
  116.5 65.0 %all-reduce.9.cloned.1.call-start = ((), (), s32[]{:S(2)}) async-start(), calls=%async_computation.6 | async-start | bytes 131072 | tf_op jit(solution)/shard_map/psum | solution.py:137
  137.7 102.6 %all-reduce.11.cloned.1.call-start = ((), (), s32[]{:S(2)}) async-start(), calls=%async_computation.7 | async-start | bytes 131072 | tf_op jit(solution)/shard_map/psum | solution.py:113
  182.4 9.2 %collective-permute-start = (bf16[16,1024]{1,0:T(8,128)(2,1)S(1)}, bf16[16,1024]{1,0:T(8,128)(2,1)S(1)}, u32[]{:S(2)}, u32[]{:S(2)}) collective-permute-start(bf16[16,1024]{1,0:T(8,128)(2,1)S(1)} %get-tuple-element.15), channel_id=1, source_target_pairs={{0,16},{1,17},{2,18},{3,19},{4,20},{5,21},{6,22},{7,23},{8,24},{9,... | collective-permute-start | bytes 98312 | tf_op jit(solution)/shard_map/ppermute | solution.py:20
  198.5 86.7 %reduce-scatter.7.cloned.1.call-start = ((), (), s32[]{:S(2)}) async-start(), calls=%async_computation.8 | async-start | bytes 327680 | tf_op jit(solution)/shard_map/reduce_scatter | solution.py:136
  256.9 72.3 %copy-start.4 = (f32[16,1024]{1,0:T(8,128)S(1)}, f32[16,1024]{1,0:T(8,128)}, u32[]{:S(2)}) copy-start(f32[16,1024]{1,0:T(8,128)} %all-reduce.11.cloned.1.call-done) | copy-start | bytes 196612
  264.1 65.1 %all-reduce.13.cloned.1.call-start = ((), (), s32[]{:S(2)}) async-start(), calls=%async_computation.9 | async-start | bytes 131072 | tf_op jit(solution)/shard_map/psum | solution.py:137
  285.3 101.3 %all-reduce.15.cloned.1.call-start = ((), (), s32[]{:S(2)}) async-start(), calls=%async_computation.10 | async-start | bytes 131072 | tf_op jit(solution)/shard_map/psum | solution.py:113
  330.1 9.3 %collective-permute-start.1 = (bf16[16,1024]{1,0:T(8,128)(2,1)S(1)}, bf16[16,1024]{1,0:T(8,128)(2,1)S(1)}, u32[]{:S(2)}, u32[]{:S(2)}) collective-permute-start(bf16[16,1024]{1,0:T(8,128)(2,1)S(1)} %get-tuple-element.11), channel_id=1, source_target_pairs={{0,16},{1,17},{2,18},{3,19},{4,20},{5,21},{6,22},{7,23},{8,24},{9,... | collective-permute-start | bytes 98312 | tf_op jit(solution)/shard_map/ppermute | solution.py:20
  340.0 3.2 copy-start.1
  344.9 86.7 %reduce-scatter.9.cloned.1.call-start = ((), (), s32[]{:S(2)}) async-start(), calls=%async_computation.11 | async-start | bytes 327680 | tf_op jit(solution)/shard_map/reduce_scatter | solution.py:136
  403.2 72.3 %copy-start.3 = (f32[16,1024]{1,0:T(8,128)S(1)}, f32[16,1024]{1,0:T(8,128)}, u32[]{:S(2)}) copy-start(f32[16,1024]{1,0:T(8,128)} %all-reduce.15.cloned.1.call-done) | copy-start | bytes 196612
  410.4 65.1 %all-reduce.17.cloned.1.call-start = ((), (), s32[]{:S(2)}) async-start(), calls=%async_computation.12 | async-start | bytes 131072 | tf_op jit(solution)/shard_map/psum | solution.py:137
  431.6 64.9 %reduce-scatter.11.cloned.1.call-start = ((), (), s32[]{:S(2)}) async-start(), calls=%async_computation.13 | async-start | bytes 327680 | tf_op jit(solution)/shard_map/reduce_scatter | solution.py:148
Sparse Core Ops, SparseCore 0:
  47.9 44.6 all-reduce.6
  116.6 21.0 reduce-scatter.4
  140.5 40.9 all-reduce.8
  198.7 41.5 all-reduce.10
  264.2 21.0 reduce-scatter.6
  288.2 40.9 all-reduce.12
  345.0 41.5 all-reduce.14
  410.6 21.0 reduce-scatter.8
  434.5 40.9 all-reduce.16
  478.1 18.4 reduce-scatter.10
where the time goes:
time: 507 us; the launch traced here: 503 us
  waiting for transfers between devices  310 us (61%)
  blocking collectives  76.8 us (15%)
  matrix products  48.3 us (10%)
  local copies, waits for them, and re-layouts  36.8 us (7%)
  other arithmetic  14 us (3%)
  between operations  13.9 us (3%)
    psum x3, waiting for transfers between devices, on_device(): mixture = lax.psum(mixture, 'head')  131 us
    psum x3, waiting for transfers between devices, on_device(): attention = lax.psum(partial_value, 'head')  96.8 us
    reduce_scatter x3, waiting for transfers between devices, on_device(): lax.psum_scatter(partial_terms, 'req', scatter_dimension=0, tiled=True)  63.4 us
    all_gather x6, blocking collectives, on_device(): lax.all_gather((normed_ffn, combine), 'req', axis=0, tiled=True)  63.3 us
    unnamed x27, local copies, waits for them, and re-layouts  25.3 us
    dot_general x3, matrix products, on_device(): jnp.dot(hidden, w_down[0], preferred_element_type=jnp.float32)  21.5 us
    reduce_scatter x1, waiting for transfers between devices, on_device(): lax.psum_scatter(placed.astype(jnp.bfloat16), 'req', scatter_dimension=0,...  18.6 us
    all_gather x1, blocking collectives, on_device(): everything = lax.all_gather(tokens, 'req', axis=0, tiled=True)  13.5 us
  transfers between devices with their start and end apart: 12, of which 10 were waited for; matrix products, arithmetic and copies ran while one was open for 3% of the time, Pallas kernels for 0%

commit v1 on v0

v1 whole, which is shorter than its diff:
```python
import functools
import math

import jax
import jax.numpy as jnp
from jax import lax
from jax.experimental import pallas as pl
from jax.experimental.pallas import tpu as pltpu
from jax.sharding import PartitionSpec as P

HEAD_DIM = 64
EXPERTS = 16
FF = 2816
LANES = 128
DEAL_LANE = EXPERTS
LENGTH_LANE = EXPERTS + 1
HEAD_ROWS = 16
MESH = pl.DeviceIdType.MESH


epsilon = 1e-06


def rms_scale(values, gain_row):
    mean_square = jnp.mean(values * values, axis=-1, keepdims=True)
    return values * lax.rsqrt(mean_square + epsilon) * gain_row


def gelu(v):
    return 0.5 * v * (1.0 + jnp.tanh(math.sqrt(2.0 / math.pi) * (v + 0.044715 * (v * v * v))))


def batched(a, b, dims):
    return lax.dot_general(a, b, (dims, ((0,), (0,))), preferred_element_type=jnp.float32)


def attend(proj, lengths, key_cache, value_cache):
    slots, context, cols = key_cache.shape
    score_scale = 1.0 / math.sqrt(HEAD_DIM)
    queries = proj[:, :cols][:, None, :]
    new_keys = proj[:, cols : 2 * cols][:, None, :]
    new_values = proj[:, 2 * cols :][:, None, :]
    row_at = lax.broadcasted_iota(jnp.int32, (1, HEAD_ROWS, cols), 1)
    lane_at = lax.broadcasted_iota(jnp.int32, (1, HEAD_ROWS, cols), 2)
    head_mask = (lane_at // HEAD_DIM == row_at).astype(jnp.float32)
    spread = queries * head_mask
    scores = batched(spread.astype(jnp.bfloat16), key_cache[...], ((2,), (2,))) * score_scale
    own_score = jnp.sum(spread * new_keys, axis=-1, keepdims=True) * score_scale
    positions = lax.broadcasted_iota(jnp.int32, (slots, HEAD_ROWS, context), 2).astype(jnp.float32)
    limit = jnp.broadcast_to(lengths, (slots, context))[:, None, :]
    scores = jnp.where(positions < limit, scores, -jnp.inf)
    peak = jnp.maximum(jnp.max(scores, axis=-1, keepdims=True), own_score)
    cache_weight = jnp.exp(scores - peak)
    own_weight = jnp.exp(own_score - peak)
    denominator = jnp.sum(cache_weight, axis=-1, keepdims=True) + own_weight
    cache_prob = (cache_weight / denominator).astype(jnp.bfloat16)
    own_prob = (own_weight / denominator).astype(jnp.bfloat16).astype(jnp.float32)
    attended = batched(cache_prob, value_cache[...], ((2,), (1,))) + own_prob * new_values
    return jnp.sum(attended * head_mask, axis=1).astype(jnp.bfloat16)


def kernel(
    req_count,
    head_count,
    meta_ref,
    tok_ref,
    again_ref,
    fgain_ref,
    wqkv_hbm,
    key_hbm,
    value_hbm,
    wout_hbm,
    wgate_hbm,
    wup_hbm,
    wdown_hbm,
    out_ref,
    wqkv,
    key_cache,
    value_cache,
    wout,
    wgate,
    wup,
    wdown,
    meta_all,
    tok_all,
    stream_in,
    stream,
    part_out,
    part_in,
    rows_all,
    rows_flat,
    total,
    terms_out,
    terms_in,
    made,
    load_sem,
    meta_sem,
    tok_sem,
    next_sem,
    head_sem,
    rows_sem,
    terms_sem,
    made_sem,
):
    sec = lax.axis_index("section")
    req = lax.axis_index("req")
    head = lax.axis_index("head")
    count = req_count * head_count
    me = req * head_count + head
    slots, width = tok_ref.shape
    own_rows = slots // head_count
    reqs = slots * req_count
    units = wgate.shape[1]
    chunk = 256 if units % 256 == 0 else units

    loads = [
        pltpu.make_async_copy(src.at[0], dst, load_sem.at[i])
        for i, (src, dst) in enumerate(
            [
                (key_hbm, key_cache),
                (value_hbm, value_cache),
                (wout_hbm, wout),
                (wgate_hbm, wgate),
                (wup_hbm, wup),
                (wdown_hbm, wdown),
            ]
        )
    ]
    load_qkv = pltpu.make_async_copy(wqkv_hbm, wqkv, load_sem.at[6])
    load_qkv.start()
    for load in loads:
        load.start()

    def peer_of(k):
        peer = lax.rem(me + k, count)
        return peer, (sec, peer // head_count, lax.rem(peer, head_count))

    def req_peer(k):
        return (sec, lax.rem(req + k, req_count), head)

    def head_peer(k):
        other = lax.rem(head + k, head_count)
        return other, (sec, req, other)

    def each(first, last, body):
        def step(k, carry):
            body(k)
            return carry

        lax.fori_loop(first, last, step, 0)

    barrier = pltpu.get_barrier_semaphore()

    def greet(k):
        _, target = peer_of(k)
        pl.semaphore_signal(barrier, inc=1, device_id=target, device_id_type=MESH)

    def greet_other(k):
        pl.semaphore_signal(barrier, inc=1, device_id=(1 - sec, req, k), device_id_type=MESH)

    each(1, count, greet)
    each(0, head_count, greet_other)
    pl.semaphore_wait(barrier, count - 1 + head_count)

    def remote(src, dst, sems, k, target):
        return pltpu.make_async_remote_copy(
            src_ref=src,
            dst_ref=dst,
            send_sem=sems.at[0, k],
            recv_sem=sems.at[1, k],
            device_id=target,
            device_id_type=MESH,
        )

    def meta_copy(k):
        return remote(meta_ref, meta_all.at[req], meta_sem, k, req_peer(k))

    def tok_copy(k):
        return remote(tok_ref, tok_all.at[req], tok_sem, k, req_peer(k))

    def next_copy(k):
        return pltpu.make_async_remote_copy(
            src_ref=made.at[me],
            dst_ref=stream_in.at[head],
            send_sem=next_sem.at[0, k],
            recv_sem=next_sem.at[1, head],
            device_id=(1, req, k),
            device_id_type=MESH,
        )

    def next_arrival(k):
        return pltpu.make_async_remote_copy(
            src_ref=made.at[me],
            dst_ref=stream_in.at[k],
            send_sem=next_sem.at[0, k],
            recv_sem=next_sem.at[1, k],
            device_id=(0, req, k),
            device_id_type=MESH,
        )

    def head_copy(k):
        other, target = head_peer(k)
        return remote(part_out.at[other], part_in.at[head], head_sem, k, target)

    def rows_copy(k):
        _, target = peer_of(k)
        return remote(rows_all.at[me], rows_all.at[me], rows_sem, k, target)

    def terms_copy(k):
        peer, target = peer_of(k)
        return remote(terms_out.at[peer], terms_in.at[me], terms_sem, k, target)

    def made_copy(k):
        _, target = peer_of(k)
        return remote(made.at[me], made.at[me], made_sem, k, target)

    @pl.when(sec == 0)
    def _():
        each(1, req_count, lambda k: tok_copy(k).start())

    each(1, req_count, lambda k: meta_copy(k).start())
    meta_all[req] = meta_ref[...]

    @pl.when(sec == 0)
    def _():
        tok_all[req] = tok_ref[...]
        each(1, req_count, lambda k: tok_copy(k).wait())
        deal = meta_ref[:, DEAL_LANE : DEAL_LANE + 1].astype(jnp.int32)
        taken = lax.broadcasted_iota(jnp.int32, (slots, reqs), 1) == deal
        dealt = jnp.dot(
            taken.astype(jnp.float32).astype(jnp.bfloat16),
            tok_all[...].reshape(reqs, width),
            preferred_element_type=jnp.float32,
        )
        stream[...] = dealt.reshape(head_count, own_rows, width)

    @pl.when(sec == 1)
    def _():
        each(0, head_count, lambda k: next_arrival(k).wait_recv())
        stream[...] = stream_in[...].astype(jnp.float32)

    normed = rms_scale(stream[...].reshape(slots, width), again_ref[...]).astype(jnp.bfloat16)
    load_qkv.wait()
    proj = jnp.dot(normed, wqkv[...], preferred_element_type=jnp.float32)
    proj = proj.astype(jnp.bfloat16).astype(jnp.float32)
    for load in loads[:3]:
        load.wait()
    attended = attend(
        proj, meta_ref[:, LENGTH_LANE : LENGTH_LANE + 1], key_cache, value_cache
    )
    partial_value = jnp.dot(attended, wout[...], preferred_element_type=jnp.float32)
    part_out[...] = partial_value.reshape(head_count, own_rows, width)
    each(1, head_count, lambda k: head_copy(k).start())
    part_in[head] = part_out[head]
    each(1, head_count, lambda k: head_copy(k).wait())
    residual = stream[head] + jnp.sum(part_in[...], axis=0)
    rows_all[me] = rms_scale(residual, fgain_ref[...]).astype(jnp.bfloat16)
    each(1, count, lambda k: rows_copy(k).start())
    each(1, req_count, lambda k: meta_copy(k).wait())
    total[...] = jnp.zeros_like(total)
    lane_at = lax.broadcasted_iota(jnp.int32, (reqs, LANES), 1)
    meta_rows = meta_all[...].reshape(reqs, LANES)
    row_weight = jnp.sum(
        jnp.where(lane_at == me * units // FF, meta_rows, 0.0), axis=1, keepdims=True
    )
    each(1, count, lambda k: rows_copy(k).wait())
    rows_flat[...] = (
        rows_all[...].astype(jnp.float32).reshape(reqs, width).astype(jnp.bfloat16)
    )
    for load in loads[3:]:
        load.wait()

    def expert(c):
        at = pl.ds(pl.multiple_of(c * chunk, chunk), chunk)
        rows = rows_flat[...]
        gate_part = jnp.dot(rows, wgate[:, at], preferred_element_type=jnp.float32)
        up_part = jnp.dot(rows, wup[:, at], preferred_element_type=jnp.float32)
        hidden = (row_weight * gelu(gate_part) * up_part).astype(jnp.bfloat16)
        total[...] += jnp.dot(hidden, wdown[at, :], preferred_element_type=jnp.float32)

    each(0, units // chunk, expert)
    terms_out[...] = total[...].reshape(count, own_rows, width).astype(jnp.bfloat16)
    each(1, count, lambda k: terms_copy(k).start())
    terms_in[me] = terms_out[me]
    each(1, count, lambda k: terms_copy(k).wait())
    mixture = jnp.sum(terms_in[...].astype(jnp.float32), axis=0)
    made[me] = (residual + mixture).astype(jnp.bfloat16)

    @pl.when(sec == 0)
    def _():
        each(0, head_count, lambda k: next_copy(k).start())

    each(1, count, lambda k: made_copy(k).start())
    each(1, count, lambda k: made_copy(k).wait())
    first = req * slots
    deal_all = meta_all[...].reshape(reqs, LANES)[:, DEAL_LANE : DEAL_LANE + 1].astype(jnp.int32)
    placed = deal_all == first + lax.broadcasted_iota(jnp.int32, (reqs, slots), 1)
    result = lax.dot_general(
        placed.astype(jnp.float32).astype(jnp.bfloat16),
        made[...].astype(jnp.float32).reshape(reqs, width).astype(jnp.bfloat16),
        (((0,), (0,)), ((), ())),
        preferred_element_type=jnp.float32,
    )
    out_ref[...] = result.astype(jnp.bfloat16)

    @pl.when(sec == 0)
    def _():
        each(0, head_count, lambda k: next_copy(k).wait_send())


def on_device(
    tokens,
    deal,
    lengths,
    cache_keys,
    cache_values,
    w_qkv,
    w_out,
    attn_gain,
    ffn_gain,
    w_gate,
    w_up,
    w_down,
    routes,
    gates,
):
    req_count = lax.axis_size("req")
    head_count = lax.axis_size("head")
    count = req_count * head_count
    slots, width = tokens.shape
    own_rows = slots // head_count
    reqs = slots * req_count
    units = w_gate.shape[2]
    cols = w_out.shape[1]
    context = cache_keys.shape[2]
    lanes = jnp.arange(LANES, dtype=jnp.int32)[None, :]
    gate_values = gates[0].astype(jnp.float32)
    meta = jnp.where(lanes == routes[0][:, 0:1], gate_values[:, 0:1], 0.0)
    meta = meta + jnp.where(lanes == routes[0][:, 1:2], gate_values[:, 1:2], 0.0)
    meta = jnp.where(lanes == DEAL_LANE, deal.astype(jnp.float32)[:, None], meta)
    meta = jnp.where(lanes == LENGTH_LANE, lengths[0].astype(jnp.float32)[:, None], meta)
    qkv_weight = w_qkv[0].reshape(width, 3 * cols)
    bf16, f32 = jnp.bfloat16, jnp.float32
    vmem = pl.BlockSpec(memory_space=pltpu.VMEM)
    anywhere = pl.BlockSpec(memory_space=pl.ANY)

    def sems(n):
        return pltpu.SemaphoreType.DMA((2, n))

    out = pl.pallas_call(
        functools.partial(kernel, req_count, head_count),
        out_shape=jax.ShapeDtypeStruct((slots, width), bf16),
        in_specs=[vmem] * 4 + [anywhere] * 7,
        out_specs=vmem,
        scratch_shapes=[
            pltpu.VMEM((width, 3 * cols), bf16),
            pltpu.VMEM((slots, context, cols), bf16),
            pltpu.VMEM((slots, context, cols), bf16),
            pltpu.VMEM((cols, width), bf16),
            pltpu.VMEM((width, units), bf16),
            pltpu.VMEM((width, units), bf16),
            pltpu.VMEM((units, width), bf16),
            pltpu.VMEM((req_count, slots, LANES), f32),
            pltpu.VMEM((req_count, slots, width), bf16),
            pltpu.VMEM((head_count, own_rows, width), bf16),
            pltpu.VMEM((head_count, own_rows, width), f32),
            pltpu.VMEM((head_count, own_rows, width), f32),
            pltpu.VMEM((head_count, own_rows, width), f32),
            pltpu.VMEM((count, own_rows, width), bf16),
            pltpu.VMEM((reqs, width), bf16),
            pltpu.VMEM((reqs, width), f32),
            pltpu.VMEM((count, own_rows, width), bf16),
            pltpu.VMEM((count, own_rows, width), bf16),
            pltpu.VMEM((count, own_rows, width), bf16),
            pltpu.SemaphoreType.DMA((7,)),
            sems(req_count),
            sems(req_count),
            sems(head_count),
            sems(head_count),
            sems(count),
            sems(count),
            sems(count),
        ],
        compiler_params=pltpu.CompilerParams(
            collective_id=0, has_side_effects=True, vmem_limit_bytes=56 * 1024 * 1024
        ),
    )(
        meta,
        tokens,
        attn_gain,
        ffn_gain,
        qkv_weight,
        cache_keys,
        cache_values,
        w_out,
        w_gate,
        w_up,
        w_down,
    )
    return out[None]


def solution(mesh):
    return jax.shard_map(
        on_device,
        mesh=mesh,
        in_specs=(
            P("req", None),
            P("req"),
            P("section", "req"),
            P("section", "req", None, "head"),
            P("section", "req", None, "head"),
            P("section", None, None, "head"),
            P("section", "head", None),
            P("section", None),
            P("section", None),
            P("section", None, ("req", "head")),
            P("section", None, ("req", "head")),
            P("section", ("req", "head"), None),
            P("section", "req", None),
            P("section", "req", None),
        ),
        out_specs=P("section", "req", None),
        check_vma=False,
    )
```

time: 507 us -> 76 us (0.15)
  waiting for transfers between devices: 310 us -> 0 us
  blocking collectives: 76.8 us -> 0 us
  Pallas kernels: 0 us -> 67.5 us
  matrix products: 48.3 us -> 0 us
  local copies, waits for them, and re-layouts: 36.8 us -> 5.54 us
  between operations: 13.9 us -> 0.02 us
  other arithmetic: 14 us -> 2.67 us
    psum x6 -> x0, waiting for transfers between devices: 228 us -> none  [the longest x3 131 us: on_device(): mixture = lax.psum(mixture, 'head')]
    reduce_scatter x4 -> x0, waiting for transfers between devices: 82 us -> none  [the longest x3 63.4 us: on_device(): lax.psum_scatter(partial_terms, 'req', scatter_dimension=0, tiled=True)]
    all_gather x7 -> x0, blocking collectives: 76.8 us -> none  [the longest x6 63.3 us: on_device(): lax.all_gather((normed_ffn, combine), 'req', axis=0, tiled=True)]
    pallas_call x0 -> x1, Pallas kernels: none -> 67.5 us  [on_device(): pl.pallas_call(functools.partial(kernel, req_count, head_count), out_shap...]
    dot_general x18 -> x0, matrix products: 48.3 us -> none  [the longest x3 21.5 us: on_device(): jnp.dot(hidden, w_down[0], preferred_element_type=jnp.float32)]
    unnamed x27 -> x2, local copies, waits for them, and re-layouts: 25.3 us -> 3.18 us
    dynamic_slice x1 -> x0, local copies, waits for them, and re-layouts: 8.89 us -> none  [on_device(): lax.dynamic_slice_in_dim(cache_values[0], row_start, block_rows, 0)]
  transfers between devices with their start and end apart: 12 -> 0, of which waited for: 10 -> 0; matrix products, arithmetic and copies ran while one was open for 3% -> 0% of each run, Pallas kernels for 0% -> 0%
where the time goes in v1:
time: 76 us; the launch traced here: 75.7 us
  Pallas kernels  67.5 us (89%)
  local copies, waits for them, and re-layouts  5.54 us (7%)
  other arithmetic  2.67 us (4%)
    pallas_call x1, Pallas kernels, on_device(): pl.pallas_call(functools.partial(kernel, req_count, head_count), out_shap...  67.5 us
    unnamed x2, local copies, waits for them, and re-layouts  3.18 us
    another operation x1, local copies, waits for them, and re-layouts, on_device(): qkv_weight = w_qkv[0].reshape(width, 3 * cols)  1.59 us

profile of v1, /device:TPU:1, one launch (start us, length us, event | category | flops | bytes accessed | tf_op | source)
XLA Modules:
  0.0 75.7 jit_solution(7094569611840606176)
XLA Ops:
  0.0 0.7 convert_element_type.21
  0.7 0.7 convert_bitcast_fusion
  1.3 0.7 bitcast_convert_fusion
  2.0 0.8 slice_bitcast_fusion.3
  2.7 0.7 select_select_fusion.meta_ref
  3.4 1.7 %copy.16 = bf16[1,1024,3,256]{1,3,2,0:T(8,128)(2,1)S(1)} copy(bf16[1,1024,3,256]{3,1,2,0:T(8,128)(2,1)} %param.19) | data formatting | bytes 3145728 | tf_op args[5]
  5.2 1.6 %copy.17.wqkv_hbm = bf16[1024,768]{1,0:T(8,128)(2,1)} copy(bf16[1024,768]{0,1:T(8,128)(2,1)S(1)} %bitcast.16) | data formatting | bytes 3145728 | tf_op jit(solution)/shard_map/reshape;squeeze | solution.py:342
  6.7 67.5 %shard_map.136 = bf16[32,1024]{1,0:T(8,128)(2,1)} custom-call(f32[32,128]{1,0:T(8,128)} %select_select_fusion.meta_ref, bf16[32,1024]{1,0:T(8,128)(2,1)} %tok_ref.1, f32[1,1024]{1,0:T(1,128)} %again_ref.1, f32[1,1024]{1,0:T(1,128)} %fgain_ref.1, bf16[1024,768]{1,0:T(8,128)(2,1)} %copy.17.wqkv_hbm, bf16[1,32,256,256]{3,2,1,0:T(8,128)(2,1)} %key_hbm.1, ...), custom_call_target="tpu_custom_call" | custom-call | tf_op jit(solution)/shard_map/pallas_call | solution.py:350
  74.3 1.5 %copy.19 = bf16[1,32,1024]{2,1,0:T(8,128)(2,1)} copy(bf16[1,32,1024]{2,1,0:T(8,128)(2,1)} %bitcast.17) | data formatting | bytes 131072
  (2 shorter events, 0.0 us)

commit v2 on v1

--- a/solution.py
+++ b/solution.py
@@ -13,8 +13,8 @@
 FF = 2816
 LANES = 128
 DEAL_LANE = EXPERTS
-LENGTH_LANE = EXPERTS + 1
 HEAD_ROWS = 16
+PARTS = 2
 MESH = pl.DeviceIdType.MESH
 
 
@@ -26,6 +26,28 @@
     return values * lax.rsqrt(mean_square + epsilon) * gain_row
 
 
+def column(row):
+    size = row.shape[1]
+    diagonal = lax.broadcasted_iota(jnp.int32, (size, size), 0) == lax.broadcasted_iota(
+        jnp.int32, (size, size), 1
+    )
+    return jnp.sum(jnp.where(diagonal, row, 0.0), axis=1, keepdims=True)
+
+
+def gathered(chosen, values):
+    return lax.dot_general(
+        chosen.astype(jnp.bfloat16),
+        values,
+        (((0,), (0,)), ((), ())),
+        preferred_element_type=jnp.float32,
+    )
+
+
+def flat(blocks):
+    count, rows, width = blocks.shape
+    return blocks[...].astype(jnp.float32).reshape(count * rows, width).astype(jnp.bfloat16)
+
+
 def gelu(v):
     return 0.5 * v * (1.0 + jnp.tanh(math.sqrt(2.0 / math.pi) * (v + 0.044715 * (v * v * v))))
 
@@ -37,9 +59,7 @@
 def attend(proj, lengths, key_cache, value_cache):
     slots, context, cols = key_cache.shape
     score_scale = 1.0 / math.sqrt(HEAD_DIM)
-    queries = proj[:, :cols][:, None, :]
-    new_keys = proj[:, cols : 2 * cols][:, None, :]
-    new_values = proj[:, 2 * cols :][:, None, :]
+    queries, new_keys, new_values = (part[:, None, :] for part in proj)
     row_at = lax.broadcasted_iota(jnp.int32, (1, HEAD_ROWS, cols), 1)
     lane_at = lax.broadcasted_iota(jnp.int32, (1, HEAD_ROWS, cols), 2)
     head_mask = (lane_at // HEAD_DIM == row_at).astype(jnp.float32)
@@ -62,7 +82,10 @@
 def kernel(
     req_count,
     head_count,
-    meta_ref,
+    deal_ref,
+    length_ref,
+    routes_ref,
+    gates_ref,
     tok_ref,
     again_ref,
     fgain_ref,
@@ -89,10 +112,14 @@
     part_in,
     rows_all,
     rows_flat,
-    total,
+    hidden,
     terms_out,
     terms_in,
     made,
+    place,
+    weights,
+    carried,
+    last,
     load_sem,
     meta_sem,
     tok_sem,
@@ -101,6 +128,7 @@
     rows_sem,
     terms_sem,
     made_sem,
+    last_sem,
 ):
     sec = lax.axis_index("section")
     req = lax.axis_index("req")
@@ -147,7 +175,11 @@
             body(k)
             return carry
 
-        lax.fori_loop(first, last, step, 0)
+        if last - first <= 16:
+            for k in range(first, last):
+                body(k)
+        else:
+            lax.fori_loop(first, last, step, 0)
 
     barrier = pltpu.get_barrier_semaphore()
 
@@ -173,7 +205,7 @@
         )
 
     def meta_copy(k):
-        return remote(meta_ref, meta_all.at[req], meta_sem, k, req_peer(k))
+        return remote(meta_all.at[req], meta_all.at[req], meta_sem, k, req_peer(k))
 
     def tok_copy(k):
         return remote(tok_ref, tok_all.at[req], tok_sem, k, req_peer(k))
@@ -206,27 +238,45 @@
         _, target = peer_of(k)
         return remote(rows_all.at[me], rows_all.at[me], rows_sem, k, target)
 
-    def terms_copy(k):
+    def terms_copy(k, part):
         peer, target = peer_of(k)
-        return remote(terms_out.at[peer], terms_in.at[me], terms_sem, k, target)
+        at = pl.ds(part * (width // PARTS), width // PARTS)
+        return remote(
+            terms_out.at[peer, :, at],
+            terms_in.at[me, :, at],
+            terms_sem,
+            part * count + k,
+            target,
+        )
 
     def made_copy(k):
         _, target = peer_of(k)
         return remote(made.at[me], made.at[me], made_sem, k, target)
 
+    def last_copy(k):
+        _, target = head_peer(k)
+        return remote(last.at[head], last.at[head], last_sem, k, target)
+
     @pl.when(sec == 0)
     def _():
         each(1, req_count, lambda k: tok_copy(k).start())
 
+    deal = column(deal_ref[...].astype(jnp.float32))
+    lengths = column(length_ref[...].astype(jnp.float32))
+    lanes = lax.broadcasted_iota(jnp.int32, (slots, LANES), 1).astype(jnp.float32)
+    meta = jnp.where(lanes == DEAL_LANE, deal, 0.0)
+    for k in range(routes_ref.shape[0]):
+        named = column(routes_ref[k : k + 1, :].astype(jnp.float32))
+        weight = column(gates_ref[...].astype(jnp.float32)[k : k + 1, :])
+        meta = meta + jnp.where(lanes == named, weight, 0.0)
+    meta_all[req] = meta
     each(1, req_count, lambda k: meta_copy(k).start())
-    meta_all[req] = meta_ref[...]
 
     @pl.when(sec == 0)
     def _():
         tok_all[req] = tok_ref[...]
         each(1, req_count, lambda k: tok_copy(k).wait())
-        deal = meta_ref[:, DEAL_LANE : DEAL_LANE + 1].astype(jnp.int32)
-        taken = lax.broadcasted_iota(jnp.int32, (slots, reqs), 1) == deal
+        taken = lax.broadcasted_iota(jnp.int32, (slots, reqs), 1) == deal.astype(jnp.int32)
         dealt = jnp.dot(
             taken.astype(jnp.float32).astype(jnp.bfloat16),
             tok_all[...].reshape(reqs, width),
@@ -241,13 +291,15 @@
 
     normed = rms_scale(stream[...].reshape(slots, width), again_ref[...]).astype(jnp.bfloat16)
     load_qkv.wait()
-    proj = jnp.dot(normed, wqkv[...], preferred_element_type=jnp.float32)
-    proj = proj.astype(jnp.bfloat16).astype(jnp.float32)
+    proj = [
+        jnp.dot(normed, wqkv[i], preferred_element_type=jnp.float32)
+        .astype(jnp.bfloat16)
+        .astype(jnp.float32)
+        for i in range(3)
+    ]
     for load in loads[:3]:
         load.wait()
-    attended = attend(
-        proj, meta_ref[:, LENGTH_LANE : LENGTH_LANE + 1], key_cache, value_cache
-    )
+    attended = attend(proj, lengths, key_cache, value_cache)
     partial_value = jnp.dot(attended, wout[...], preferred_element_type=jnp.float32)
     part_out[...] = partial_value.reshape(head_count, own_rows, width)
     each(1, head_count, lambda k: head_copy(k).start())
@@ -257,55 +309,90 @@
     rows_all[me] = rms_scale(residual, fgain_ref[...]).astype(jnp.bfloat16)
     each(1, count, lambda k: rows_copy(k).start())
     each(1, req_count, lambda k: meta_copy(k).wait())
-    total[...] = jnp.zeros_like(total)
     lane_at = lax.broadcasted_iota(jnp.int32, (reqs, LANES), 1)
     meta_rows = meta_all[...].reshape(reqs, LANES)
+    deal_all = meta_rows[:, DEAL_LANE : DEAL_LANE + 1].astype(jnp.int32)
+
+    @pl.when(sec == 0)
+    def _():
+        weights[...] = meta_rows
+
+    @pl.when(sec == 1)
+    def _():
+        slot_to = deal_all == lax.broadcasted_iota(jnp.int32, (reqs, reqs), 1)
+        place[...] = slot_to.astype(jnp.float32).reshape(count, own_rows, reqs)
+        weights[...] = gathered(
+            place[...].reshape(reqs, reqs), meta_rows.astype(jnp.bfloat16)
+        )
+        high = residual.astype(jnp.bfloat16)
+        rest = residual - high.astype(jnp.float32)
+        middle = rest.astype(jnp.bfloat16)
+        low = (rest - middle.astype(jnp.float32)).astype(jnp.bfloat16)
+        mine = place[me]
+        carried[...] = gathered(mine, high) + gathered(mine, middle) + gathered(mine, low)
+
     row_weight = jnp.sum(
-        jnp.where(lane_at == me * units // FF, meta_rows, 0.0), axis=1, keepdims=True
+        jnp.where(lane_at == me * units // FF, weights[...], 0.0), axis=1, keepdims=True
     )
     each(1, count, lambda k: rows_copy(k).wait())
-    rows_flat[...] = (
-        rows_all[...].astype(jnp.float32).reshape(reqs, width).astype(jnp.bfloat16)
-    )
+
+    @pl.when(sec == 0)
+    def _():
+        rows_flat[...] = flat(rows_all)
+
+    @pl.when(sec == 1)
+    def _():
+        rows_flat[...] = gathered(place[...].reshape(reqs, reqs), flat(rows_all)).astype(
+            jnp.bfloat16
+        )
+
     for load in loads[3:]:
         load.wait()
 
-    def expert(c):
-        at = pl.ds(pl.multiple_of(c * chunk, chunk), chunk)
+    def hide(c):
+        at = pl.ds(c * chunk, chunk)
         rows = rows_flat[...]
         gate_part = jnp.dot(rows, wgate[:, at], preferred_element_type=jnp.float32)
         up_part = jnp.dot(rows, wup[:, at], preferred_element_type=jnp.float32)
-        hidden = (row_weight * gelu(gate_part) * up_part).astype(jnp.bfloat16)
-        total[...] += jnp.dot(hidden, wdown[at, :], preferred_element_type=jnp.float32)
-
-    each(0, units // chunk, expert)
-    terms_out[...] = total[...].reshape(count, own_rows, width).astype(jnp.bfloat16)
-    each(1, count, lambda k: terms_copy(k).start())
+        hidden[:, at] = (row_weight * gelu(gate_part) * up_part).astype(jnp.bfloat16)
+
+    for c in range(units // chunk):
+        hide(c)
+    for part in range(PARTS):
+        at = pl.ds(part * (width // PARTS), width // PARTS)
+        done = jnp.dot(hidden[...], wdown[:, at], preferred_element_type=jnp.float32)
+
+        @pl.when(sec == 0)
+        def _():
+            terms_out[:, :, at] = done.reshape(count, own_rows, -1).astype(jnp.bfloat16)
+
+        @pl.when(sec == 1)
+        def _():
+            with_residual = done + carried[:, at]
+            terms_out[:, :, at] = with_residual.reshape(count, own_rows, -1).astype(jnp.bfloat16)
+
+        each(1, count, lambda k: terms_copy(k, part).start())
     terms_in[me] = terms_out[me]
-    each(1, count, lambda k: terms_copy(k).wait())
+    for part in range(PARTS):
+        each(1, count, lambda k: terms_copy(k, part).wait())
     mixture = jnp.sum(terms_in[...].astype(jnp.float32), axis=0)
-    made[me] = (residual + mixture).astype(jnp.bfloat16)
 
     @pl.when(sec == 0)
     def _():
+        made[me] = (residual + mixture).astype(jnp.bfloat16)
         each(0, head_count, lambda k: next_copy(k).start())
-
-    each(1, count, lambda k: made_copy(k).start())
-    each(1, count, lambda k: made_copy(k).wait())
-    first = req * slots
-    deal_all = meta_all[...].reshape(reqs, LANES)[:, DEAL_LANE : DEAL_LANE + 1].astype(jnp.int32)
-    placed = deal_all == first + lax.broadcasted_iota(jnp.int32, (reqs, slots), 1)
-    result = lax.dot_general(
-        placed.astype(jnp.float32).astype(jnp.bfloat16),
-        made[...].astype(jnp.float32).reshape(reqs, width).astype(jnp.bfloat16),
-        (((0,), (0,)), ((), ())),
-        preferred_element_type=jnp.float32,
-    )
-    out_ref[...] = result.astype(jnp.bfloat16)
-
-    @pl.when(sec == 0)
-    def _():
+        each(1, count, lambda k: made_copy(k).start())
+        each(1, count, lambda k: made_copy(k).wait())
+        placed = deal_all == req * slots + lax.broadcasted_iota(jnp.int32, (reqs, slots), 1)
+        out_ref[...] = gathered(placed.astype(jnp.float32), flat(made))
         each(0, head_count, lambda k: next_copy(k).wait_send())
+
+    @pl.when(sec == 1)
+    def _():
+        last[head] = mixture.astype(jnp.bfloat16)
+        each(1, head_count, lambda k: last_copy(k).start())
+        each(1, head_count, lambda k: last_copy(k).wait())
+        out_ref[...] = last[...].astype(jnp.float32).reshape(slots, width)
 
 
 def on_device(
@@ -333,13 +420,7 @@
     units = w_gate.shape[2]
     cols = w_out.shape[1]
     context = cache_keys.shape[2]
-    lanes = jnp.arange(LANES, dtype=jnp.int32)[None, :]
-    gate_values = gates[0].astype(jnp.float32)
-    meta = jnp.where(lanes == routes[0][:, 0:1], gate_values[:, 0:1], 0.0)
-    meta = meta + jnp.where(lanes == routes[0][:, 1:2], gate_values[:, 1:2], 0.0)
-    meta = jnp.where(lanes == DEAL_LANE, deal.astype(jnp.float32)[:, None], meta)
-    meta = jnp.where(lanes == LENGTH_LANE, lengths[0].astype(jnp.float32)[:, None], meta)
-    qkv_weight = w_qkv[0].reshape(width, 3 * cols)
+    qkv_weight = w_qkv[0].transpose(1, 0, 2)
     bf16, f32 = jnp.bfloat16, jnp.float32
     vmem = pl.BlockSpec(memory_space=pltpu.VMEM)
     anywhere = pl.BlockSpec(memory_space=pl.ANY)
@@ -349,11 +430,11 @@
 
     out = pl.pallas_call(
         functools.partial(kernel, req_count, head_count),
-        out_shape=jax.ShapeDtypeStruct((slots, width), bf16),
-        in_specs=[vmem] * 4 + [anywhere] * 7,
+        out_shape=jax.ShapeDtypeStruct((slots, width), f32),
+        in_specs=[vmem] * 7 + [anywhere] * 7,
         out_specs=vmem,
         scratch_shapes=[
-            pltpu.VMEM((width, 3 * cols), bf16),
+            pltpu.VMEM((3, width, cols), bf16),
             pltpu.VMEM((slots, context, cols), bf16),
             pltpu.VMEM((slots, context, cols), bf16),
             pltpu.VMEM((cols, width), bf16),
@@ -368,24 +449,32 @@
             pltpu.VMEM((head_count, own_rows, width), f32),
             pltpu.VMEM((count, own_rows, width), bf16),
             pltpu.VMEM((reqs, width), bf16),
-            pltpu.VMEM((reqs, width), f32),
+            pltpu.VMEM((reqs, units), bf16),
             pltpu.VMEM((count, own_rows, width), bf16),
             pltpu.VMEM((count, own_rows, width), bf16),
             pltpu.VMEM((count, own_rows, width), bf16),
+            pltpu.VMEM((count, own_rows, reqs), f32),
+            pltpu.VMEM((reqs, LANES), f32),
+            pltpu.VMEM((reqs, width), f32),
+            pltpu.VMEM((head_count, own_rows, width), bf16),
             pltpu.SemaphoreType.DMA((7,)),
             sems(req_count),
             sems(req_count),
             sems(head_count),
             sems(head_count),
             sems(count),
+            sems(PARTS * count),
             sems(count),
-            sems(count),
+            sems(head_count),
         ],
         compiler_params=pltpu.CompilerParams(
             collective_id=0, has_side_effects=True, vmem_limit_bytes=56 * 1024 * 1024
         ),
     )(
-        meta,
+        deal[None],
+        lengths,
+        routes[0].T,
+        gates[0].T,
         tokens,
         attn_gain,
         ffn_gain,
@@ -397,7 +486,7 @@
         w_up,
         w_down,
     )
-    return out[None]
+    return out.astype(bf16)[None]
 
 
 def solution(mesh):

time: 76 us -> 60.7 us (0.80)
  Pallas kernels: 67.5 us -> 58.9 us
  local copies, waits for them, and re-layouts: 5.54 us -> 0 us
  other arithmetic: 2.67 us -> 1.54 us
    pallas_call x1, Pallas kernels: 67.5 us -> 58.9 us  [on_device(): pl.pallas_call(functools.partial(kernel, req_count, head_count), out_shap...]
    unnamed x2 -> x0, local copies, waits for them, and re-layouts: 3.18 us -> none
    convert_element_type x3 -> x0, other arithmetic: 1.97 us -> none  [the longest x1 0.66 us: on_device(): deal.astype(jnp.float32)[:, None]]
    another operation x1 -> x0, local copies, waits for them, and re-layouts: 1.59 us -> none  [on_device(): qkv_weight = w_qkv[0].reshape(width, 3 * cols)]
    broadcast_in_dim x0 -> x1, other arithmetic: none -> 1.54 us  [on_device(): return out.astype(bf16)[None]]
where the time goes in v2:
time: 60.7 us; the launch traced here: 60.5 us
  Pallas kernels  58.9 us (97%)
  other arithmetic  1.54 us (3%)
    pallas_call x1, Pallas kernels, on_device(): pl.pallas_call(functools.partial(kernel, req_count, head_count), out_shap...  58.9 us
    broadcast_in_dim x1, other arithmetic, on_device(): return out.astype(bf16)[None]  1.54 us

profile of v2, /device:TPU:1, one launch (start us, length us, event | category | flops | bytes accessed | tf_op | source)
XLA Modules:
  0.0 60.5 jit_solution(15543702044857020807)
XLA Ops:
  0.0 58.9 %shard_map.136 = f32[32,1024]{1,0:T(8,128)} custom-call(s32[1,32]{1,0:T(1,128)} %bitcast.14, s32[1,32]{1,0:T(1,128)} %length_ref.1, s32[2,32]{1,0:T(2,128)} %bitcast.13, bf16[2,32]{1,0:T(2,128)(2,1)} %bitcast.15, bf16[32,1024]{1,0:T(8,128)(2,1)} %tok_ref.1, f32[1,1024]{1,0:T(1,128)} %again_ref.1, f32[1,1024]{1,0:T(1,128)} %fgain_ref.1, ...), custom_call_target="tpu_custom_call" | custom-call | tf_op jit(solution)/shard_map/pallas_call | solution.py:431
  58.9 1.5 %convert_bitcast_fusion = bf16[1,32,1024]{2,1,0:T(8,128)(2,1)} fusion(f32[32,1024]{1,0:T(8,128)} %shard_map.136), kind=kLoop, calls=%fused_computation | loop fusion | flops 32768 | bytes 196608 | tf_op jit(solution)/shard_map/broadcast_in_dim | solution.py:489

commit v3 on v2

--- a/solution.py
+++ b/solution.py
@@ -381,11 +381,11 @@
     def _():
         made[me] = (residual + mixture).astype(jnp.bfloat16)
         each(0, head_count, lambda k: next_copy(k).start())
+        each(0, head_count, lambda k: next_copy(k).wait_send())
         each(1, count, lambda k: made_copy(k).start())
         each(1, count, lambda k: made_copy(k).wait())
         placed = deal_all == req * slots + lax.broadcasted_iota(jnp.int32, (reqs, slots), 1)
         out_ref[...] = gathered(placed.astype(jnp.float32), flat(made))
-        each(0, head_count, lambda k: next_copy(k).wait_send())
 
     @pl.when(sec == 1)
     def _():

time: 60.7 us -> 60.4 us (level)
  no operation moved by 1% of the time
where the time goes in v3:
time: 60.4 us; the launch traced here: 60.2 us
  Pallas kernels  58.6 us (97%)
  other arithmetic  1.54 us (3%)
    pallas_call x1, Pallas kernels, on_device(): pl.pallas_call(functools.partial(kernel, req_count, head_count), out_shap...  58.6 us
    broadcast_in_dim x1, other arithmetic, on_device(): return out.astype(bf16)[None]  1.54 us

profile of v3, /device:TPU:1, one launch (start us, length us, event | category | flops | bytes accessed | tf_op | source)
XLA Modules:
  0.0 60.2 jit_solution(15000518705001770700)
XLA Ops:
  0.0 58.6 %shard_map.136 = f32[32,1024]{1,0:T(8,128)} custom-call(s32[1,32]{1,0:T(1,128)} %bitcast.14, s32[1,32]{1,0:T(1,128)} %length_ref.1, s32[2,32]{1,0:T(2,128)} %bitcast.13, bf16[2,32]{1,0:T(2,128)(2,1)} %bitcast.15, bf16[32,1024]{1,0:T(8,128)(2,1)} %tok_ref.1, f32[1,1024]{1,0:T(1,128)} %again_ref.1, f32[1,1024]{1,0:T(1,128)} %fgain_ref.1, ...), custom_call_target="tpu_custom_call" | custom-call | tf_op jit(solution)/shard_map/pallas_call | solution.py:431
  58.6 1.5 %convert_bitcast_fusion = bf16[1,32,1024]{2,1,0:T(8,128)(2,1)} fusion(f32[32,1024]{1,0:T(8,128)} %shard_map.136), kind=kLoop, calls=%fused_computation | loop fusion | flops 32768 | bytes 196608 | tf_op jit(solution)/shard_map/broadcast_in_dim | solution.py:489
